TPU v7x, 32 devices: a whole 2x2x4 slice. The times are simulated.
32 devices in a mesh: grp: 2 (over x), reg: 16 (over z, y, core).
Axes of the slice: x: 2, y: 2, z: 4, core: 2. Of those that a mesh axis runs over, the one named last changes fastest.
Arguments:
- waveforms: bfloat16 [32, 3, 4096], P('grp', None, 'reg'), parts along dimension 0, may hold values from -6 to 6
- tail: bfloat16 [32, 3, 768], P('grp'), parts along dimension 0, may hold values from -6 to 6
- station_lists: int32 [32, 4], P('grp'), parts along dimension 0, may hold values from 0 to 15
- station_count: int32 [32], P(('grp', 'reg')), parts along dimension 0, may hold values from 1 to 4, 48 in all
- bank_of_region: int32 [32], P(('grp', 'reg')), parts along dimension 0, may hold values from 0 to 7
- library: bfloat16 [8, 16, 12, 512], replicated, may hold values from -0.25 to 0.25
- moveouts: int32 [32, 16, 12], P(('grp', 'reg')), parts along dimension 0, may hold values from 0 to 2
Outputs:
- detection: float32 [32, 4096], P('grp', 'reg'), parts along dimension 0
There are 2 independent parts, one for each index of `grp`. A program takes and returns all parts, laid end to end along the dimension named above; an argument that names none is the same for every part. Nothing has to cross between parts.
All inputs are finite; a program needn't handle non-finite values. No bound on the sum of `station_count` on one device may be relied on, other than what follows from the above.
Results may differ from a plain program's by a relative error of at most 0.0003.
Values may be sent and summed in bfloat16 or wider, within the bound.
A program may use at most 64 MiB of HBM per device.

v0:
```python
import functools
import math

import jax
import jax.numpy as jnp
from jax import lax
from jax.experimental import pallas as pl
from jax.experimental.pallas import tpu as pltpu
from jax.sharding import PartitionSpec as P

UNIT = 128
PAIRS = 4


def exchange_kernel(n, wave_ref, tail_ref, mov_ref, count_ref, bank_ref, rec_ref, meta_ref,
                    mine, halo_send, halo_recv, meta_send, meta_recv):
    me = lax.axis_index("reg")
    piece = wave_ref.shape[2]
    halos = tail_ref.shape[2] // piece
    channels, _, templates = mov_ref.shape

    mine[...] = jnp.zeros_like(mine)
    for c in range(channels):
        mine[c:c + 1, 0:templates] = mov_ref[c]
    mine[channels:channels + 1] = jnp.full((1, mine.shape[1]), count_ref[0], jnp.int32)
    mine[channels + 1:channels + 2] = jnp.full((1, mine.shape[1]), bank_ref[0], jnp.int32)

    barrier = pltpu.get_barrier_semaphore()

    @pl.loop(1, n)
    def _(step):
        pl.semaphore_signal(barrier, inc=1, device_id={"reg": lax.rem(me + step, n)},
                            device_id_type=pl.DeviceIdType.MESH)

    pl.semaphore_wait(barrier, n - 1)

    def halo_copy(h):
        return pltpu.make_async_remote_copy(
            src_ref=wave_ref,
            dst_ref=rec_ref.at[:, :, pl.ds(h * piece, piece)],
            send_sem=halo_send.at[h - 1],
            recv_sem=halo_recv.at[h - 1],
            device_id={"reg": lax.rem(me + n - h, n)},
            device_id_type=pl.DeviceIdType.MESH,
        )

    for h in range(1, halos + 1):
        @pl.when(me >= h)
        def _():
            halo_copy(h).start()

    def meta_copy(step):
        return pltpu.make_async_remote_copy(
            src_ref=mine,
            dst_ref=meta_ref.at[me],
            send_sem=meta_send.at[step],
            recv_sem=meta_recv.at[step],
            device_id={"reg": lax.rem(me + step, n)},
            device_id_type=pl.DeviceIdType.MESH,
        )

    @pl.loop(1, n)
    def _(step):
        meta_copy(step).start()

    meta_ref[me] = mine[...]
    rec_ref[:, :, 0:piece] = wave_ref[...]
    for h in range(1, halos + 1):
        for q in range(h):
            @pl.when(me + h - n == q)
            def _():
                rec_ref[:, :, h * piece:(h + 1) * piece] = tail_ref[:, :, q * piece:(q + 1) * piece]

    for h in range(1, halos + 1):
        @pl.when(me >= h)
        def _():
            halo_copy(h).wait_send()

        @pl.when(me + h < n)
        def _():
            halo_copy(h).wait_recv()

    @pl.loop(1, n)
    def _(step):
        meta_copy(step).wait_send()
        meta_copy(step).wait_recv()


def exchange(n, waveforms, tail, moveouts, station_count, bank_of_region):
    comps, stations, piece = waveforms.shape
    height = -(-(moveouts.shape[0] + 2) // 8) * 8
    halos = tail.shape[2] // piece
    vmem = pl.BlockSpec(memory_space=pltpu.VMEM)
    smem = pl.BlockSpec(memory_space=pltpu.SMEM)
    return pl.pallas_call(
        functools.partial(exchange_kernel, n),
        out_shape=(
            jax.ShapeDtypeStruct((comps, stations, piece + tail.shape[2]), waveforms.dtype),
            jax.ShapeDtypeStruct((n, height, 128), jnp.int32),
        ),
        in_specs=[vmem, vmem, vmem, smem, smem],
        out_specs=(vmem, vmem),
        scratch_shapes=[
            pltpu.VMEM((height, 128), jnp.int32),
            pltpu.SemaphoreType.DMA((halos,)),
            pltpu.SemaphoreType.DMA((halos,)),
            pltpu.SemaphoreType.DMA((n,)),
            pltpu.SemaphoreType.DMA((n,)),
        ],
        compiler_params=pltpu.CompilerParams(collective_id=0, has_side_effects=True,
                                             vmem_limit_bytes=32 << 20),
        name="exchange",
    )(waveforms, tail, moveouts, station_count, bank_of_region)


def stack_kernel(taps, piece, scale, lists_ref, scal_ref, rec_ref, lib_hbm, mov_ref, out_ref,
                 lib_ref, hank0, hank1, fans, gain, pairs, place, lib_sem):
    comps, stations, record = rec_ref.shape
    slots, regions = lists_ref.shape
    channels = slots * comps
    templates = lib_ref.shape[1]
    moves = (record - piece - taps) // UNIT + 1
    width = piece + (moves - 1) * UNIT
    deep = 2 * UNIT
    reach = width + taps - deep
    rows = comps * stations

    lib_copy = pltpu.make_async_copy(lib_hbm, lib_ref, lib_sem)
    lib_copy.start()

    @pl.loop(0, stations + 1)
    def _(s):
        place[s] = 0

    @pl.loop(0, regions)
    def _(r):
        @pl.loop(0, scal_ref[r, 0])
        def _(k):
            s = lists_ref[k, r]
            place[s + 1] = place[s + 1] + 1

    @pl.loop(0, stations)
    def _(s):
        place[s + 1] = place[s + 1] + place[s]

    @pl.loop(0, regions)
    def _(r):
        @pl.loop(0, scal_ref[r, 0])
        def _(k):
            s = lists_ref[k, r]
            pairs[place[s]] = r * slots + k
            place[s] = place[s] + 1

    @pl.loop(0, stations, step=16)
    def _(s):
        s = pl.multiple_of(s, 16)
        for c in range(comps):
            x = rec_ref[c, pl.ds(s, 16)].astype(jnp.float32)
            for k in range(8):
                at = pl.multiple_of(k * rows + c * stations + s, 16)
                moved = pltpu.roll(x, record - k, 1) if k else x
                for j in range(fans.shape[0]):
                    fans[j, pl.ds(at, 16)] = moved[:, j * UNIT:(j + 1) * UNIT]
            window = x * x
            span = 1
            while span < taps:
                window = window + pltpu.roll(window, record - span, 1)
                span *= 2
            at = pl.multiple_of(c * stations + s, 16)
            gain[pl.ds(at, 16)] = lax.rsqrt(window[:, 0:width] / taps + 1e-05) * scale

    out_ref[...] = jnp.zeros_like(out_ref)
    diagonal = (lax.broadcasted_iota(jnp.int32, (templates, UNIT), 0)
                == lax.broadcasted_iota(jnp.int32, (templates, UNIT), 1))

    def build(s, hank):
        for c in range(comps):
            fan = jnp.concatenate([fans[j, pl.ds(c * stations + s, 8, stride=rows)]
                                   for j in range(fans.shape[0])], axis=1)
            fan = jnp.concatenate([fan, pltpu.roll(fan, record - 8, 1)], axis=0).astype(jnp.bfloat16)
            for g in range(0, UNIT, 16):
                both = (pltpu.roll(fan, record - g, 1) if g else fan).astype(jnp.bfloat16)
                hank[c, g:g + 16] = both[:, 0:reach]
                hank[c, UNIT + g:UNIT + g + 16] = both[:, UNIT:UNIT + reach]

    def chunk(s, first, end, hank):
        picks = []
        for p in range(PAIRS):
            at = jnp.maximum(jnp.minimum(first + p, end - 1), 0)
            pair = pairs[at]
            r = pair // slots
            channel = (pair - r * slots) * comps
            picks.append((r, scal_ref[r, 1] * channels + channel, channel,
                          jnp.where(first + p < end, 0, moves)))
        total = jnp.zeros(out_ref.shape, jnp.float32)
        for c in range(comps):
            kernels = jnp.concatenate([lib_ref[base + c] for _, base, _, _ in picks], axis=0)
            corr = None
            for d in range(taps // deep):
                term = jnp.dot(kernels[:, d * deep:(d + 1) * deep],
                               hank[c, :, d * deep:d * deep + width],
                               preferred_element_type=jnp.float32)
                corr = term if corr is None else corr + term
            corr = corr * gain[pl.ds(c * stations + s, 1)]
            for p, (r, _, channel, dead) in enumerate(picks):
                mine = corr[p * templates:(p + 1) * templates]
                delays = jnp.broadcast_to(mov_ref[r, pl.ds(channel + c, 1)], diagonal.shape)
                shift = jnp.sum(jnp.where(diagonal, delays, 0), axis=1, keepdims=True) + dead
                for m in range(moves):
                    total = total + jnp.where(shift == m, mine[:, m * UNIT:m * UNIT + piece], 0.0)
        return total

    def process(s, hank, other):
        end = place[s]
        begin = jnp.where(s == 0, 0, place[jnp.maximum(s - 1, 0)])
        total = chunk(s, begin, end, hank)
        build(jnp.minimum(s + 1, stations - 1), other)
        out_ref[...] += total

        @pl.loop(1, pl.cdiv(end - begin, PAIRS))
        def _(q):
            out_ref[...] += chunk(s, begin + q * PAIRS, end, hank)

    build(0, hank0)
    lib_copy.wait()

    @pl.loop(0, stations, step=2)
    def _(s):
        process(s, hank0, hank1)
        process(s + 1, hank1, hank0)


def stack(taps, piece, scale, lists, scal, record, bank_rows, meta):
    slots, regions = lists.shape
    comps, stations, samples = record.shape
    templates = bank_rows.shape[1]
    width = samples - taps
    vmem = pl.BlockSpec(memory_space=pltpu.VMEM)
    smem = pl.BlockSpec(memory_space=pltpu.SMEM)
    signal = pltpu.VMEM((comps, 2 * UNIT, width + taps - 2 * UNIT), jnp.bfloat16)
    return pl.pallas_call(
        functools.partial(stack_kernel, taps, piece, scale),
        out_shape=jax.ShapeDtypeStruct((templates, piece), jnp.float32),
        in_specs=[smem, smem, vmem, pl.BlockSpec(memory_space=pltpu.HBM), vmem],
        out_specs=vmem,
        scratch_shapes=[
            pltpu.VMEM(bank_rows.shape, bank_rows.dtype),
            signal,
            signal,
            pltpu.VMEM((samples // UNIT, 8 * comps * stations, UNIT), jnp.float32),
            pltpu.VMEM((comps * stations, width), jnp.float32),
            pltpu.SMEM((regions * slots,), jnp.int32),
            pltpu.SMEM((stations + 1,), jnp.int32),
            pltpu.SemaphoreType.DMA,
        ],
        compiler_params=pltpu.CompilerParams(vmem_limit_bytes=40 << 20),
        name="stack",
    )(lists, scal, record, bank_rows, meta)


def on_device(waveforms, tail, station_lists, station_count, bank_of_region, library, moveouts):
    regions = lax.axis_size("reg")
    comps, piece = waveforms.shape[1:]
    banks, templates, channels, taps = library.shape
    slots = station_lists.shape[1]
    scale = 1.0 / math.sqrt(comps * slots * regions)
    bank_rows = jnp.transpose(library, (0, 2, 1, 3)).reshape(banks * channels, templates, taps)
    record, meta = exchange(regions, jnp.transpose(waveforms, (1, 0, 2)), jnp.transpose(tail, (1, 0, 2)),
                            jnp.transpose(moveouts, (2, 0, 1)), station_count, bank_of_region)
    scal = meta[:, channels:channels + 2, 0]
    return stack(taps, piece, scale, station_lists.T, scal, record, bank_rows, meta)


def solution(mesh):
    return jax.shard_map(
        on_device,
        mesh=mesh,
        in_specs=(
            P("grp", None, "reg"),
            P("grp", None, None),
            P("grp", None),
            P(("grp", "reg")),
            P(("grp", "reg")),
            P(),
            P(("grp", "reg"), None, None),
        ),
        out_specs=P("grp", "reg"),
        check_vma=False,
    )
```

profile of v0, /device:TPU:0, one launch (start us, length us, event | category | flops | bytes accessed | tf_op | source)
XLA Modules:
  0.0 34.1 jit_solution(14066497259048671167)
XLA Ops:
  1.3 0.0 copy-start.1
  1.3 0.9 %copy-done.1 = bf16[16,3,768]{2,0,1:T(8,128)(2,1)S(1)} copy-done((bf16[16,3,768]{2,0,1:T(8,128)(2,1)S(1)}, bf16[16,3,768]{2,0,1:T(8,128)(2,1)}, u32[]{:S(2)}) %copy-start.1) | copy-done | bytes 73752
  2.2 0.0 copy-start.2
  2.2 0.7 %copy-done.2 = bf16[16,3,256]{2,0,1:T(8,128)(2,1)S(1)} copy-done((bf16[16,3,256]{2,0,1:T(8,128)(2,1)S(1)}, bf16[16,3,256]{2,0,1:T(8,128)(2,1)}, u32[]{:S(2)}) %copy-start.2) | copy-done | bytes 24600
  2.9 0.0 copy-start.3
  2.9 0.7 %copy-done.3 = s32[1,16,12]{1,0,2:T(1,128)S(1)} copy-done((s32[1,16,12]{1,0,2:T(1,128)S(1)}, s32[1,16,12]{1,0,2:T(1,128)}, u32[]{:S(2)}) %copy-start.3) | copy-done | bytes 792
  3.6 11.6 %exchange.1 = (bf16[3,16,1024]{2,1,0:T(8,128)(2,1)S(1)}, s32[16,16,128]{2,1,0:T(8,128)S(1)}) custom-call(bf16[3,16,256]{2,1,0:T(8,128)(2,1)S(1)} %bitcast.10, bf16[3,16,768]{2,1,0:T(8,128)(2,1)S(1)} %bitcast.9, s32[12,1,16]{2,1,0:T(1,128)S(1)} %bitcast.11, s32[1]{0:T(128)S(6)} %copy.10.count_ref, s32[1]{0:T(128)S(6)} %copy.11.bank_ref), custom_call_target="tpu_custom_call" | custom-call | tf_op jit(solution)/shard_map/exchange/pallas_call | solution.py:95
  15.2 0.1 copy.8
  15.3 0.1 copy.9.scal_ref
  15.4 0.0 copy-start
  15.4 1.4 %copy-done = bf16[8,16,12,512]{3,1,2,0:T(8,128)(2,1)S(1)} copy-done((bf16[8,16,12,512]{3,1,2,0:T(8,128)(2,1)S(1)}, bf16[8,16,12,512]{3,1,2,0:T(8,128)(2,1)}, u32[]{:S(2)}) %copy-start) | copy-done | bytes 1572888
  16.8 0.0 copy-start.4
  16.8 0.7 %copy-done.4 = s32[16,4]{0,1:T(4,128)S(1)} copy-done((s32[16,4]{0,1:T(4,128)S(1)}, s32[16,4]{0,1:T(4,128)}, u32[]{:S(2)}) %copy-start.4) | copy-done | bytes 280
  17.5 16.6 %stack.1 = f32[16,256]{1,0:T(8,128)} custom-call(s32[4,16]{1,0:T(4,128)S(1)} %bitcast.12, s32[16,2]{1,0:T(8,128)S(1)} %copy.9.scal_ref, bf16[3,16,1024]{2,1,0:T(8,128)(2,1)S(1)} %get-tuple-element.8.rec_ref, bf16[96,16,512]{2,1,0:T(8,128)(2,1)S(1)} %bitcast.8, s32[16,16,128]{2,1,0:T(8,128)S(1)} %get-tuple-element.7.mov_ref), custom_call_target="tpu_custom_call" | custom-call | tf_op jit(solution)/shard_map/stack/pallas_call | solution.py:241
  (1 shorter events, 0.0 us)
Async XLA Ops:
  1.3 0.9 %copy-start.1 = (bf16[16,3,768]{2,0,1:T(8,128)(2,1)S(1)}, bf16[16,3,768]{2,0,1:T(8,128)(2,1)}, u32[]{:S(2)}) copy-start(bf16[16,3,768]{2,0,1:T(8,128)(2,1)} %param.8) | copy-start | bytes 221188
  2.2 0.7 %copy-start.2 = (bf16[16,3,256]{2,0,1:T(8,128)(2,1)S(1)}, bf16[16,3,256]{2,0,1:T(8,128)(2,1)}, u32[]{:S(2)}) copy-start(bf16[16,3,256]{2,0,1:T(8,128)(2,1)} %param.7) | copy-start | bytes 73732
  2.9 0.7 %copy-start.3 = (s32[1,16,12]{1,0,2:T(1,128)S(1)}, s32[1,16,12]{1,0,2:T(1,128)}, u32[]{:S(2)}) copy-start(s32[1,16,12]{1,0,2:T(1,128)} %param.13) | copy-start | bytes 2308
  15.4 1.4 %copy-start = (bf16[8,16,12,512]{3,1,2,0:T(8,128)(2,1)S(1)}, bf16[8,16,12,512]{3,1,2,0:T(8,128)(2,1)}, u32[]{:S(2)}) copy-start(bf16[8,16,12,512]{3,1,2,0:T(8,128)(2,1)} %param.12) | copy-start | bytes 4718596
  16.8 0.7 %copy-start.4 = (s32[16,4]{0,1:T(4,128)S(1)}, s32[16,4]{0,1:T(4,128)}, u32[]{:S(2)}) copy-start(s32[16,4]{0,1:T(4,128)} %param.9) | copy-start | bytes 772
where the time goes:
time: 34.2 us; the launch traced here: 34.1 us
  Pallas kernels  28.2 us (82%)
  local copies, waits for them, and re-layouts  4.58 us (13%)
  between operations  1.33 us (4%)
    pallas_call x1, Pallas kernels, stack(): pl.pallas_call(functools.partial(stack_kernel, taps, piece, scale), out_s...  16.6 us
    pallas_call x1, Pallas kernels, exchange(): pl.pallas_call(functools.partial(exchange_kernel, n), out_shape=(jax.Shap...  11.6 us
    unnamed x10, local copies, waits for them, and re-layouts  4.4 us

commit v1 on v0

--- a/solution.py
+++ b/solution.py
@@ -9,7 +9,7 @@
 from jax.sharding import PartitionSpec as P
 
 UNIT = 128
-PAIRS = 4
+PAIRS = 8
 
 
 def exchange_kernel(n, wave_ref, tail_ref, mov_ref, count_ref, bank_ref, rec_ref, meta_ref,
@@ -108,7 +108,7 @@
             pltpu.SemaphoreType.DMA((n,)),
         ],
         compiler_params=pltpu.CompilerParams(collective_id=0, has_side_effects=True,
-                                             vmem_limit_bytes=32 << 20),
+                                             vmem_limit_bytes=62 << 20),
         name="exchange",
     )(waveforms, tail, moveouts, station_count, bank_of_region)
 
@@ -241,7 +241,7 @@
     return pl.pallas_call(
         functools.partial(stack_kernel, taps, piece, scale),
         out_shape=jax.ShapeDtypeStruct((templates, piece), jnp.float32),
-        in_specs=[smem, smem, vmem, pl.BlockSpec(memory_space=pltpu.HBM), vmem],
+        in_specs=[smem, smem, vmem, pl.BlockSpec(memory_space=pl.ANY), vmem],
         out_specs=vmem,
         scratch_shapes=[
             pltpu.VMEM(bank_rows.shape, bank_rows.dtype),
@@ -253,7 +253,7 @@
             pltpu.SMEM((stations + 1,), jnp.int32),
             pltpu.SemaphoreType.DMA,
         ],
-        compiler_params=pltpu.CompilerParams(vmem_limit_bytes=40 << 20),
+        compiler_params=pltpu.CompilerParams(vmem_limit_bytes=62 << 20),
         name="stack",
     )(lists, scal, record, bank_rows, meta)
 

time: 34.2 us -> 31.7 us (0.927)
  local copies, waits for them, and re-layouts: 4.58 us -> 1.62 us
    unnamed x10 -> x0, local copies, waits for them, and re-layouts: 4.4 us -> none
    pallas_call x1, Pallas kernels: 11.6 us -> 13.1 us  [exchange(): pl.pallas_call(functools.partial(exchange_kernel, n), out_shape=(jax.Shap...]
    pallas_call x1, Pallas kernels: 16.6 us -> 15.5 us  [stack(): pl.pallas_call(functools.partial(stack_kernel, taps, piece, scale), out_s...]
    slice x2, local copies, waits for them, and re-layouts: 0.1 us -> 0.94 us  [on_device(): scal = meta[:, channels:channels + 2, 0]]
    squeeze x1, local copies, waits for them, and re-layouts: 0.09 us -> 0.68 us  [on_device(): scal = meta[:, channels:channels + 2, 0]]
where the time goes in v1:
time: 31.7 us; the launch traced here: 31.5 us
  Pallas kernels  28.5 us (90%)
  local copies, waits for them, and re-layouts  1.62 us (5%)
  between operations  1.31 us (4%)
    pallas_call x1, Pallas kernels, stack(): pl.pallas_call(functools.partial(stack_kernel, taps, piece, scale), out_s...  15.5 us
    pallas_call x1, Pallas kernels, exchange(): pl.pallas_call(functools.partial(exchange_kernel, n), out_shape=(jax.Shap...  13.1 us
    slice x2, local copies, waits for them, and re-layouts, on_device(): scal = meta[:, channels:channels + 2, 0]  0.94 us
    squeeze x1, local copies, waits for them, and re-layouts, on_device(): scal = meta[:, channels:channels + 2, 0]  0.68 us

profile of v1, /device:TPU:0, one launch (start us, length us, event | category | flops | bytes accessed | tf_op | source)
XLA Modules:
  0.0 31.5 jit_solution(15651952033096841291)
XLA Ops:
  1.3 13.1 %exchange.1 = (bf16[3,16,1024]{2,1,0:T(8,128)(2,1)}, s32[16,16,128]{2,1,0:T(8,128)}) custom-call(bf16[3,16,256]{2,1,0:T(8,128)(2,1)} %bitcast.10, bf16[3,16,768]{2,1,0:T(8,128)(2,1)} %bitcast.9, s32[12,1,16]{2,1,0:T(1,128)} %bitcast.11, s32[1]{0:T(128)S(6)} %copy.10.count_ref, s32[1]{0:T(128)S(6)} %copy.11.bank_ref), custom_call_target="tpu_custom_call" | custom-call | tf_op jit(solution)/shard_map/exchange/pallas_call | solution.py:95
  14.4 0.8 %slice.3 = s32[16,2,1]{2,1,0:T(2,128)S(1)} slice(s32[16,16,128]{2,1,0:T(8,128)} %get-tuple-element.7.mov_ref), slice={[0:16], [12:14], [0:1]} | slice | bytes 256 | tf_op jit(solution)/shard_map/slice | solution.py:270
  15.2 0.1 copy.8
  15.3 0.7 %copy.9.scal_ref = s32[16,2]{1,0:T(8,128)} copy(s32[16,2]{0,1:T(2,128)S(1)} %bitcast.12) | data formatting | bytes 256 | tf_op jit(solution)/shard_map/squeeze | solution.py:270
  16.0 15.5 %stack.1 = f32[16,256]{1,0:T(8,128)} custom-call(s32[4,16]{1,0:T(4,128)} %bitcast.13, s32[16,2]{1,0:T(8,128)} %copy.9.scal_ref, bf16[3,16,1024]{2,1,0:T(8,128)(2,1)} %get-tuple-element.8.rec_ref, bf16[96,16,512]{2,1,0:T(8,128)(2,1)} %bitcast.8, s32[16,16,128]{2,1,0:T(8,128)} %get-tuple-element.7.mov_ref), custom_call_target="tpu_custom_call" | custom-call | tf_op jit(solution)/shard_map/stack/pallas_call | solution.py:241

commit v2 on v1

--- a/solution.py
+++ b/solution.py
@@ -113,8 +113,8 @@
     )(waveforms, tail, moveouts, station_count, bank_of_region)
 
 
-def stack_kernel(taps, piece, scale, lists_ref, scal_ref, rec_ref, lib_hbm, mov_ref, out_ref,
-                 lib_ref, hank0, hank1, fans, gain, pairs, place, lib_sem):
+def stack_kernel(taps, piece, scale, lists_ref, rec_ref, lib_hbm, mov_ref, out_ref,
+                 lib_ref, hank0, hank1, fans, gain, pairs, place, scal_ref, lib_sem, scal_sem):
     comps, stations, record = rec_ref.shape
     slots, regions = lists_ref.shape
     channels = slots * comps
@@ -127,29 +127,10 @@
 
     lib_copy = pltpu.make_async_copy(lib_hbm, lib_ref, lib_sem)
     lib_copy.start()
-
-    @pl.loop(0, stations + 1)
-    def _(s):
-        place[s] = 0
-
-    @pl.loop(0, regions)
-    def _(r):
-        @pl.loop(0, scal_ref[r, 0])
-        def _(k):
-            s = lists_ref[k, r]
-            place[s + 1] = place[s + 1] + 1
-
-    @pl.loop(0, stations)
-    def _(s):
-        place[s + 1] = place[s + 1] + place[s]
-
-    @pl.loop(0, regions)
-    def _(r):
-        @pl.loop(0, scal_ref[r, 0])
-        def _(k):
-            s = lists_ref[k, r]
-            pairs[place[s]] = r * slots + k
-            place[s] = place[s] + 1
+    facts = channels // 8 * 8
+    scal_copy = pltpu.make_async_copy(mov_ref.at[:, facts:facts + 8, :], scal_ref, scal_sem)
+
+    scal_copy.start()
 
     @pl.loop(0, stations, step=16)
     def _(s):
@@ -169,6 +150,31 @@
             at = pl.multiple_of(c * stations + s, 16)
             gain[pl.ds(at, 16)] = lax.rsqrt(window[:, 0:width] / taps + 1e-05) * scale
 
+    scal_copy.wait()
+    for s in range(stations + 1):
+        place[s] = 0
+
+    @pl.loop(0, regions)
+    def _(r):
+        count = scal_ref[r, channels - facts, 0]
+        for k in range(slots):
+            s = lists_ref[k, r]
+            place[s + 1] = place[s + 1] + jnp.where(k < count, 1, 0)
+
+    @pl.loop(0, stations)
+    def _(s):
+        place[s + 1] = place[s + 1] + place[s]
+
+    @pl.loop(0, regions)
+    def _(r):
+        count = scal_ref[r, channels - facts, 0]
+        for k in range(slots):
+            s = lists_ref[k, r]
+            at = place[s]
+            live = k < count
+            pairs[jnp.where(live, at, regions * slots)] = r * slots + k
+            place[s] = at + jnp.where(live, 1, 0)
+
     out_ref[...] = jnp.zeros_like(out_ref)
     diagonal = (lax.broadcasted_iota(jnp.int32, (templates, UNIT), 0)
                 == lax.broadcasted_iota(jnp.int32, (templates, UNIT), 1))
@@ -190,7 +196,7 @@
             pair = pairs[at]
             r = pair // slots
             channel = (pair - r * slots) * comps
-            picks.append((r, scal_ref[r, 1] * channels + channel, channel,
+            picks.append((r, scal_ref[r, channels - facts + 1, 0] * channels + channel, channel,
                           jnp.where(first + p < end, 0, moves)))
         total = jnp.zeros(out_ref.shape, jnp.float32)
         for c in range(comps):
@@ -230,7 +236,7 @@
         process(s + 1, hank1, hank0)
 
 
-def stack(taps, piece, scale, lists, scal, record, bank_rows, meta):
+def stack(taps, piece, scale, lists, record, bank_rows, meta):
     slots, regions = lists.shape
     comps, stations, samples = record.shape
     templates = bank_rows.shape[1]
@@ -241,7 +247,7 @@
     return pl.pallas_call(
         functools.partial(stack_kernel, taps, piece, scale),
         out_shape=jax.ShapeDtypeStruct((templates, piece), jnp.float32),
-        in_specs=[smem, smem, vmem, pl.BlockSpec(memory_space=pl.ANY), vmem],
+        in_specs=[smem, vmem, pl.BlockSpec(memory_space=pl.ANY), vmem],
         out_specs=vmem,
         scratch_shapes=[
             pltpu.VMEM(bank_rows.shape, bank_rows.dtype),
@@ -249,13 +255,15 @@
             signal,
             pltpu.VMEM((samples // UNIT, 8 * comps * stations, UNIT), jnp.float32),
             pltpu.VMEM((comps * stations, width), jnp.float32),
-            pltpu.SMEM((regions * slots,), jnp.int32),
+            pltpu.SMEM((regions * slots + 1,), jnp.int32),
             pltpu.SMEM((stations + 1,), jnp.int32),
+            pltpu.SMEM((regions, 8, meta.shape[2]), jnp.int32),
+            pltpu.SemaphoreType.DMA,
             pltpu.SemaphoreType.DMA,
         ],
         compiler_params=pltpu.CompilerParams(vmem_limit_bytes=62 << 20),
         name="stack",
-    )(lists, scal, record, bank_rows, meta)
+    )(lists, record, bank_rows, meta)
 
 
 def on_device(waveforms, tail, station_lists, station_count, bank_of_region, library, moveouts):
@@ -267,8 +275,7 @@
     bank_rows = jnp.transpose(library, (0, 2, 1, 3)).reshape(banks * channels, templates, taps)
     record, meta = exchange(regions, jnp.transpose(waveforms, (1, 0, 2)), jnp.transpose(tail, (1, 0, 2)),
                             jnp.transpose(moveouts, (2, 0, 1)), station_count, bank_of_region)
-    scal = meta[:, channels:channels + 2, 0]
-    return stack(taps, piece, scale, station_lists.T, scal, record, bank_rows, meta)
+    return stack(taps, piece, scale, station_lists.T, record, bank_rows, meta)
 
 
 def solution(mesh):

time: 31.7 us -> 29.7 us (0.937)
  local copies, waits for them, and re-layouts: 1.62 us -> 0 us
    slice x2 -> x0, local copies, waits for them, and re-layouts: 0.94 us -> none  [on_device(): scal = meta[:, channels:channels + 2, 0]]
    squeeze x1 -> x0, local copies, waits for them, and re-layouts: 0.68 us -> none  [on_device(): scal = meta[:, channels:channels + 2, 0]]
    pallas_call x1, Pallas kernels: 15.5 us -> 15.1 us  [stack(): pl.pallas_call(functools.partial(stack_kernel, taps, piece, scale), out_s...]
where the time goes in v2:
time: 29.7 us; the launch traced here: 29.5 us
  Pallas kernels  28.2 us (95%)
  between operations  1.3 us (4%)
    pallas_call x1, Pallas kernels, stack(): pl.pallas_call(functools.partial(stack_kernel, taps, piece, scale), out_s...  15.1 us
    pallas_call x1, Pallas kernels, exchange(): pl.pallas_call(functools.partial(exchange_kernel, n), out_shape=(jax.Shap...  13.1 us

profile of v2, /device:TPU:0, one launch (start us, length us, event | category | flops | bytes accessed | tf_op | source)
XLA Modules:
  0.0 29.5 jit_solution(8568481995698061226)
XLA Ops:
  1.3 13.1 %exchange.1 = (bf16[3,16,1024]{2,1,0:T(8,128)(2,1)}, s32[16,16,128]{2,1,0:T(8,128)}) custom-call(bf16[3,16,256]{2,1,0:T(8,128)(2,1)} %bitcast.9, bf16[3,16,768]{2,1,0:T(8,128)(2,1)} %bitcast.8, s32[12,1,16]{2,1,0:T(1,128)} %bitcast.10, s32[1]{0:T(128)S(6)} %copy.8.count_ref, s32[1]{0:T(128)S(6)} %copy.9.bank_ref), custom_call_target="tpu_custom_call" | custom-call | tf_op jit(solution)/shard_map/exchange/pallas_call | solution.py:95
  14.4 15.1 %stack.1 = f32[16,256]{1,0:T(8,128)} custom-call(s32[4,16]{1,0:T(4,128)} %bitcast.11, bf16[3,16,1024]{2,1,0:T(8,128)(2,1)} %get-tuple-element.7.rec_ref, bf16[96,16,512]{2,1,0:T(8,128)(2,1)} %bitcast.7, s32[16,16,128]{2,1,0:T(8,128)} %get-tuple-element.8.mov_ref), custom_call_target="tpu_custom_call" | custom-call | tf_op jit(solution)/shard_map/stack/pallas_call | solution.py:247

commit v3 on v2

--- a/solution.py
+++ b/solution.py
@@ -13,7 +13,7 @@
 
 
 def exchange_kernel(n, wave_ref, tail_ref, mov_ref, count_ref, bank_ref, rec_ref, meta_ref,
-                    mine, halo_send, halo_recv, meta_send, meta_recv):
+                    mine, local, halo_send, halo_recv, meta_send, meta_recv):
     me = lax.axis_index("reg")
     piece = wave_ref.shape[2]
     halos = tail_ref.shape[2] // piece
@@ -24,6 +24,23 @@
         mine[c:c + 1, 0:templates] = mov_ref[c]
     mine[channels:channels + 1] = jnp.full((1, mine.shape[1]), count_ref[0], jnp.int32)
     mine[channels + 1:channels + 2] = jnp.full((1, mine.shape[1]), bank_ref[0], jnp.int32)
+
+    own_copies = [
+        pltpu.make_async_copy(wave_ref, rec_ref.at[:, :, pl.ds(0, piece)], local.at[0]),
+        pltpu.make_async_copy(mine, meta_ref.at[me], local.at[1]),
+    ]
+
+    def tail_copy(h, q):
+        return pltpu.make_async_copy(tail_ref.at[:, :, pl.ds(q * piece, piece)],
+                                     rec_ref.at[:, :, pl.ds(h * piece, piece)], local.at[h + 1])
+
+    for copy in own_copies:
+        copy.start()
+    for h in range(1, halos + 1):
+        for q in range(h):
+            @pl.when(me + h - n == q)
+            def _():
+                tail_copy(h, q).start()
 
     barrier = pltpu.get_barrier_semaphore()
 
@@ -63,15 +80,14 @@
     def _(step):
         meta_copy(step).start()
 
-    meta_ref[me] = mine[...]
-    rec_ref[:, :, 0:piece] = wave_ref[...]
+    for copy in own_copies:
+        copy.wait()
     for h in range(1, halos + 1):
         for q in range(h):
             @pl.when(me + h - n == q)
             def _():
-                rec_ref[:, :, h * piece:(h + 1) * piece] = tail_ref[:, :, q * piece:(q + 1) * piece]
-
-    for h in range(1, halos + 1):
+                tail_copy(h, q).wait()
+
         @pl.when(me >= h)
         def _():
             halo_copy(h).wait_send()
@@ -91,6 +107,7 @@
     height = -(-(moveouts.shape[0] + 2) // 8) * 8
     halos = tail.shape[2] // piece
     vmem = pl.BlockSpec(memory_space=pltpu.VMEM)
+    anywhere = pl.BlockSpec(memory_space=pl.ANY)
     smem = pl.BlockSpec(memory_space=pltpu.SMEM)
     return pl.pallas_call(
         functools.partial(exchange_kernel, n),
@@ -98,10 +115,11 @@
             jax.ShapeDtypeStruct((comps, stations, piece + tail.shape[2]), waveforms.dtype),
             jax.ShapeDtypeStruct((n, height, 128), jnp.int32),
         ),
-        in_specs=[vmem, vmem, vmem, smem, smem],
-        out_specs=(vmem, vmem),
+        in_specs=[anywhere, anywhere, vmem, smem, smem],
+        out_specs=(anywhere, anywhere),
         scratch_shapes=[
             pltpu.VMEM((height, 128), jnp.int32),
+            pltpu.SemaphoreType.DMA((halos + 2,)),
             pltpu.SemaphoreType.DMA((halos,)),
             pltpu.SemaphoreType.DMA((halos,)),
             pltpu.SemaphoreType.DMA((n,)),

time: 29.7 us -> 29.3 us (0.987)
  Pallas kernels: 28.2 us -> 27.8 us
    pallas_call x1, Pallas kernels: 13.1 us -> 12.6 us  [exchange(): pl.pallas_call(functools.partial(exchange_kernel, n), out_shape=(jax.Shap...]
where the time goes in v3:
time: 29.3 us; the launch traced here: 29.1 us
  Pallas kernels  27.8 us (95%)
  between operations  1.3 us (4%)
    pallas_call x1, Pallas kernels, stack(): pl.pallas_call(functools.partial(stack_kernel, taps, piece, scale), out_s...  15.1 us
    pallas_call x1, Pallas kernels, exchange(): pl.pallas_call(functools.partial(exchange_kernel, n), out_shape=(jax.Shap...  12.6 us

profile of v3, /device:TPU:0, one launch (start us, length us, event | category | flops | bytes accessed | tf_op | source)
XLA Modules:
  0.0 29.1 jit_solution(3476931870801467124)
XLA Ops:
  1.3 12.6 %exchange.1 = (bf16[3,16,1024]{2,1,0:T(8,128)(2,1)}, s32[16,16,128]{2,1,0:T(8,128)}) custom-call(bf16[3,16,256]{2,1,0:T(8,128)(2,1)} %bitcast.9, bf16[3,16,768]{2,1,0:T(8,128)(2,1)} %bitcast.8, s32[12,1,16]{2,1,0:T(1,128)} %bitcast.10, s32[1]{0:T(128)S(6)} %copy.8.count_ref, s32[1]{0:T(128)S(6)} %copy.9.bank_ref), custom_call_target="tpu_custom_call" | custom-call | tf_op jit(solution)/shard_map/exchange/pallas_call | solution.py:112
  13.9 15.1 %stack.1 = f32[16,256]{1,0:T(8,128)} custom-call(s32[4,16]{1,0:T(4,128)} %bitcast.11, bf16[3,16,1024]{2,1,0:T(8,128)(2,1)} %get-tuple-element.7.rec_ref, bf16[96,16,512]{2,1,0:T(8,128)(2,1)} %bitcast.7, s32[16,16,128]{2,1,0:T(8,128)} %get-tuple-element.8.mov_ref), custom_call_target="tpu_custom_call" | custom-call | tf_op jit(solution)/shard_map/stack/pallas_call | solution.py:265
